TPU v7x, 32 devices: a whole 2x2x4 slice. The times are simulated.
32 devices in a mesh: expert: 8 (over z, y), dp: 4 (over x, core).
Axes of the slice: x: 2, y: 2, z: 4, core: 2. Of those that a mesh axis runs over, the one named last changes fastest.
Arguments:
- tokens: bfloat16 [4096, 1440], P(('expert', 'dp')), may hold values from -6 to 6
- routes: int32 [4096, 4], P(('expert', 'dp')), may hold values from 0 to 7, as said below
- gate_fixed: int32 [4096, 4], P(('expert', 'dp')), may hold values from 4096 to 65535
- counts: int32 [32], P(('expert', 'dp')), may hold values from 32 to 128, as said below
- replica_plan: int32 [4], replicated, may hold values from 0 to 7, as said below
- weight_in: bfloat16 [8, 1440, 1440], P('expert', None, 'dp'), may hold values from -0.15625 to 0.15625
- weight_out: bfloat16 [8, 1440, 1440], P('expert', 'dp'), may hold values from -0.15625 to 0.15625
- cotangent: bfloat16 [4096, 1440], P(('expert', 'dp')), may hold values from -0.59765625 to 0.59765625
Outputs:
- layer_output: bfloat16 [4096, 1440], P(('expert', 'dp'))
- input_grads: bfloat16 [4096, 1440], P(('expert', 'dp'))
- weight_in_grad: bfloat16 [8, 1440, 1440], P('expert', None, 'dp')
- weight_out_grad: bfloat16 [8, 1440, 1440], P('expert', 'dp')
Inputs may be any that keep to these rules, and one draw needn't show every extreme that they name: `routes`: each row names 4 different experts. `replica_plan`: 4 different experts, among them 0, 3, 4 and 7, in any order. `counts`: some device has 128 live tokens in every draw.
All inputs are finite; a program needn't handle non-finite values.
Results may differ from a plain program's by a relative error of at most 0.0064.
Values may be sent and summed in bfloat16 or wider, within the bound.
A program may use at most 128 MiB of HBM per device.

v0:
```python
import jax
import jax.numpy as jnp
from jax import lax
from jax.sharding import PartitionSpec as P


def shifted(value, axis, steps):
    count = lax.axis_size(axis)
    pairs = [(source, (source + steps) % count) for source in range(count)]
    return lax.ppermute(value, axis, pairs)


def activate(values):
    return values * jax.nn.sigmoid(1.702 * values)


def derivative(values):
    sigmoid_value = jax.nn.sigmoid(1.702 * values)
    return sigmoid_value + 1.702 * values * sigmoid_value * (1.0 - sigmoid_value)


def slot_tables(routes, live_count, frequent_indicator, experts, capacity, spare_slots):
    token_count, top_count = routes.shape
    slot_width = capacity + spare_slots
    active = (jnp.arange(token_count, dtype=jnp.int32) < live_count).astype(jnp.int32)
    flattened = routes.reshape(-1)
    active_flat = jnp.repeat(active, top_count, total_repeat_length=token_count * top_count)
    same_expert = (flattened[:, None] == jnp.arange(experts, dtype=jnp.int32)[None, :]).astype(
        jnp.int32
    )
    matches = same_expert * active_flat[:, None]
    before = jnp.cumsum(matches, axis=0) - matches
    position = jnp.sum(before * matches, axis=1)
    hot_route = jnp.sum(same_expert * frequent_indicator[None, :], axis=1)
    keep_route = (active_flat > 0) & (position < capacity + spare_slots * hot_route)
    target_block = jnp.where(position < capacity, flattened, (flattened + experts // 2) % experts)
    slot_index = jnp.where(keep_route, target_block * slot_width + position, experts * slot_width)
    source = jnp.full((experts * slot_width + 1,), -1, jnp.int32)
    source = source.at[slot_index].set(jnp.arange(token_count * top_count, dtype=jnp.int32))
    return (slot_index, source[: experts * slot_width])


def gather_back(returned, slot_index, features):
    flattened = returned.reshape(-1, features)
    padded = jnp.concatenate([flattened, jnp.zeros((1, features), flattened.dtype)], axis=0)
    return padded[slot_index].astype(jnp.float32)


def slot_products(stacked, own_weight, copy_weight, dims, capacity, amount):
    width = stacked.shape[2]
    own_part = stacked[:, :capacity].reshape(-1, width)
    copy_part = stacked[:, capacity:].reshape(-1, width)
    own_term = lax.dot_general(own_part, own_weight, dims, preferred_element_type=jnp.float32)
    copy_term = lax.dot_general(copy_part, copy_weight, dims, preferred_element_type=jnp.float32)
    return jnp.concatenate(
        [
            own_term.reshape(amount, capacity, -1),
            copy_term.reshape(amount, stacked.shape[1] - capacity, -1),
        ],
        axis=1,
    )


def on_device(tokens, routes, gate_fixed, counts, replica_plan, weight_in, weight_out, cotangent):
    token_count, features = tokens.shape
    top_count = routes.shape[1]
    groups = lax.axis_size("expert")
    experts = groups * weight_in.shape[0]
    capacity = 3 * token_count * top_count // (8 * experts)
    spare_slots = capacity // 2
    slot_width = capacity + spare_slots
    contract_first = (((0,), (0,)), ((), ()))
    contract_last = (((1,), (1,)), ((), ()))
    contract_plain = (((1,), (0,)), ((), ()))
    frequent_indicator = jnp.sum(
        (replica_plan[:, None] == jnp.arange(experts, dtype=jnp.int32)[None, :]).astype(jnp.int32),
        axis=0,
    )
    slot_index, source = slot_tables(
        routes, counts[0], frequent_indicator, experts, capacity, spare_slots
    )
    filled = (source >= 0)[:, None]
    route_ids = jnp.maximum(source, 0)
    token_ids = route_ids // top_count
    scales = gate_fixed.reshape(-1).astype(jnp.float32) / 65536.0
    sent_rows = jnp.where(filled, tokens[token_ids], jnp.zeros((), jnp.bfloat16)).reshape(
        experts, slot_width, features
    )
    grad_rows = jnp.where(
        filled, scales[route_ids][:, None] * cotangent[token_ids].astype(jnp.float32), 0.0
    )
    grad_rows = grad_rows.astype(jnp.bfloat16).reshape(experts, slot_width, features)
    slab_in, slab_out = shifted((weight_in, weight_out), "expert", groups // 2)
    w_first = weight_in[0]
    w_second = weight_out[0]
    copy_first = slab_in[0]
    copy_second = slab_out[0]
    inbound = lax.all_to_all(sent_rows, "expert", split_axis=0, concat_axis=0, tiled=True)
    all_in = lax.all_gather(inbound, "dp", axis=0, tiled=True)
    blocks = all_in.shape[0]
    own_rows = all_in[:, :capacity].reshape(-1, features)
    copy_rows = all_in[:, capacity:].reshape(-1, features)
    own_pre = jnp.dot(own_rows, w_first, preferred_element_type=jnp.float32)
    copy_pre = jnp.dot(copy_rows, copy_first, preferred_element_type=jnp.float32)
    own_act = activate(own_pre).astype(jnp.bfloat16)
    copy_act = activate(copy_pre).astype(jnp.bfloat16)
    hidden_share = own_act.shape[1]
    act_all = jnp.concatenate(
        [
            own_act.reshape(blocks, capacity, hidden_share),
            copy_act.reshape(blocks, spare_slots, hidden_share),
        ],
        axis=1,
    )
    outputs = lax.psum_scatter(
        slot_products(
            act_all, w_second, copy_second, contract_plain, capacity, groups * lax.axis_size("dp")
        ),
        "dp",
        scatter_dimension=0,
        tiled=True,
    ).astype(jnp.bfloat16)
    returned = lax.all_to_all(outputs, "expert", split_axis=0, concat_axis=0, tiled=True)
    inbound_grad = lax.all_to_all(grad_rows, "expert", split_axis=0, concat_axis=0, tiled=True)
    all_grad = lax.all_gather(inbound_grad, "dp", axis=0, tiled=True)
    own_grad = all_grad[:, :capacity].reshape(-1, features)
    copy_grad = all_grad[:, capacity:].reshape(-1, features)
    own_act_grad = lax.dot_general(
        own_grad, w_second, contract_last, preferred_element_type=jnp.float32
    )
    copy_act_grad = lax.dot_general(
        copy_grad, copy_second, contract_last, preferred_element_type=jnp.float32
    )
    own_pre_grad = (own_act_grad * derivative(own_pre)).astype(jnp.bfloat16)
    copy_pre_grad = (copy_act_grad * derivative(copy_pre)).astype(jnp.bfloat16)
    pre_all = jnp.concatenate(
        [
            own_pre_grad.reshape(blocks, capacity, hidden_share),
            copy_pre_grad.reshape(blocks, spare_slots, hidden_share),
        ],
        axis=1,
    )
    input_rows = lax.psum_scatter(
        slot_products(
            pre_all, w_first, copy_first, contract_last, capacity, groups * lax.axis_size("dp")
        ),
        "dp",
        scatter_dimension=0,
        tiled=True,
    ).astype(jnp.bfloat16)
    copy_term_second = lax.dot_general(
        copy_act, copy_grad, contract_first, preferred_element_type=jnp.float32
    )
    copy_term_first = lax.dot_general(
        copy_rows, copy_pre_grad, contract_first, preferred_element_type=jnp.float32
    )
    home_second, home_first = (
        shifted(copy_term_second.astype(jnp.bfloat16), "expert", groups // 2).astype(
            copy_term_second.dtype
        ),
        shifted(copy_term_first.astype(jnp.bfloat16), "expert", groups // 2).astype(
            copy_term_first.dtype
        ),
    )
    grad_second = (
        lax.dot_general(own_act, own_grad, contract_first, preferred_element_type=jnp.float32)
        + home_second
    )
    grad_first = (
        lax.dot_general(own_rows, own_pre_grad, contract_first, preferred_element_type=jnp.float32)
        + home_first
    )
    weight_out_grad = grad_second.astype(jnp.bfloat16)[None]
    weight_in_grad = grad_first.astype(jnp.bfloat16)[None]
    returned_grad = lax.all_to_all(input_rows, "expert", split_axis=0, concat_axis=0, tiled=True)
    picked = gather_back(returned, slot_index, features) * scales[:, None]
    layer_output = jnp.sum(picked.reshape(token_count, top_count, features), axis=1).astype(
        jnp.bfloat16
    )
    picked_grad = gather_back(returned_grad, slot_index, features)
    input_grads = jnp.sum(picked_grad.reshape(token_count, top_count, features), axis=1).astype(
        jnp.bfloat16
    )
    return (layer_output, input_grads, weight_in_grad, weight_out_grad)


def solution(mesh):
    return jax.shard_map(
        on_device,
        mesh=mesh,
        in_specs=(
            P(("expert", "dp"), None),
            P(("expert", "dp"), None),
            P(("expert", "dp"), None),
            P(("expert", "dp")),
            P(),
            P("expert", None, "dp"),
            P("expert", "dp", None),
            P(("expert", "dp"), None),
        ),
        out_specs=(
            P(("expert", "dp"), None),
            P(("expert", "dp"), None),
            P("expert", None, "dp"),
            P("expert", "dp", None),
        ),
        check_vma=False,
    )
```

profile of v0, /device:TPU:0, one launch (start us, length us, event | category | flops | bytes accessed | tf_op | source)
XLA Modules:
  0.0 436.9 jit_solution(12339639959429125588)
XLA Ops:
  8.7 3.3 gather_fusion
  14.3 2.4 scatter_custom_fusion
  17.1 2.2 gather_fusion.1
  19.7 31.5 %all_to_all.20 = bf16[8,36,1440]{2,1,0:T(8,128)(2,1)S(1)} all-to-all(bf16[8,36,1440]{2,1,0:T(8,128)(2,1)S(1)} %broadcast_select_fusion), channel_id=1, replica_groups=mesh['expert'=8,'dp'=4] {'expert'}, dimensions={0} | all-to-all | bytes 1658880 | tf_op jit(solution)/shard_map/all_to_all | solution.py:98
  52.7 2.4 gather_fusion.3
  55.4 2.2 gather_fusion.4
  58.0 27.5 %all_to_all.21 = bf16[8,36,1440]{2,1,0:T(8,128)(2,1)S(1)} all-to-all(bf16[8,36,1440]{2,1,0:T(8,128)(2,1)S(1)} %select_convert_fusion), channel_id=1, replica_groups=mesh['expert'=8,'dp'=4] {'expert'}, dimensions={0} | all-to-all | bytes 1658880 | tf_op jit(solution)/shard_map/all_to_all | solution.py:124
  88.1 1.9 collective-permute-start.1
  90.0 1.7 slice-done
  91.7 2.7 copy.85
  94.4 1.4 slice-done.1
  97.0 64.1 %collective-permute-done = bf16[1,1440,360]{2,1,0:T(8,128)(2,1)} collective-permute-done((bf16[1,1440,360]{2,1,0:T(8,128)(2,1)}, bf16[1,1440,360]{2,1,0:T(8,128)(2,1)}, u32[]{:S(2)}, u32[]{:S(2)}) %collective-permute-start) | collective-permute-done | bytes 1036832 | tf_op jit(solution)/shard_map/ppermute | solution.py:10
  161.2 2.9 multiply_convert_fusion.1
  164.4 20.0 %collective-permute-done.1 = bf16[1,360,1440]{2,1,0:T(8,128)(2,1)} collective-permute-done((bf16[1,360,1440]{2,1,0:T(8,128)(2,1)}, bf16[1,360,1440]{2,1,0:T(8,128)(2,1)}, u32[]{:S(2)}, u32[]{:S(2)}) %collective-permute-start.1) | collective-permute-done | bytes 1036832 | tf_op jit(solution)/shard_map/ppermute | solution.py:10
  184.4 2.0 fusion.8
  186.4 1.4 copy.90
  188.0 3.6 multiply_convert_fusion
  191.6 2.1 copy.86
  193.7 2.8 fusion.13
  196.5 4.1 pad_maximum_fusion
  201.0 1.7 slice-done.2
  202.6 2.8 copy.95
  205.4 1.6 slice-done.3
  208.3 3.2 fusion.1
  212.6 2.1 fusion.4
  214.7 1.4 copy.100
  216.8 3.2 fusion
  220.1 2.1 copy.96
  222.2 3.3 fusion.6
  225.5 4.2 pad_maximum_fusion.1
  229.7 39.4 %reduce-scatter.3.cloned.1.call-done = f32[8,36,1440]{2,1,0:T(8,128)} async-done(((f32[32,36,1440]{2,1,0:T(8,128)}), f32[8,36,1440]{2,1,0:T(8,128)}) %reduce-scatter.3.cloned.1.call-update) | async-done | bytes 1658896 | tf_op jit(solution)/shard_map/reduce_scatter | solution.py:115
  269.1 2.6 convert_element_type.79
  271.7 5.6 %all-to-all-start.1 = ((bf16[8,36,1440]{2,1,0:T(8,128)(2,1)}), bf16[8,36,1440]{2,1,0:T(8,128)(2,1)S(1)}, u32[]{:S(2)}, u32[]{:S(2)}) async-start(bf16[8,36,1440]{2,1,0:T(8,128)(2,1)} %convert_element_type.79), calls=%async_computation.2 | async-start | bytes 1966080 | tf_op jit(solution)/shard_map/all_to_all | solution.py:123
  278.2 3.0 collective-permute-start.3
  282.6 58.4 %reduce-scatter.5.cloned.1.call-done = f32[8,36,1440]{2,1,0:T(8,128)} async-done(((f32[32,36,1440]{2,1,0:T(8,128)}), f32[8,36,1440]{2,1,0:T(8,128)}) %reduce-scatter.5.cloned.1.call-update) | async-done | bytes 1658896 | tf_op jit(solution)/shard_map/reduce_scatter | solution.py:143
  341.1 2.6 convert_element_type.89
  343.7 6.8 %all-to-all-done.1 = bf16[8,36,1440]{2,1,0:T(8,128)(2,1)S(1)} async-done(((bf16[8,36,1440]{2,1,0:T(8,128)(2,1)}), bf16[8,36,1440]{2,1,0:T(8,128)(2,1)S(1)}, u32[]{:S(2)}, u32[]{:S(2)}) %all-to-all-start.1) | async-done | bytes 829472 | tf_op jit(solution)/shard_map/all_to_all | solution.py:123
  350.5 4.5 %all-to-all-start.3 = ((bf16[8,36,1440]{2,1,0:T(8,128)(2,1)}), bf16[8,36,1440]{2,1,0:T(8,128)(2,1)}, u32[]{:S(2)}, u32[]{:S(2)}) async-start(bf16[8,36,1440]{2,1,0:T(8,128)(2,1)} %convert_element_type.89), calls=%async_computation.5 | async-start | bytes 1966080 | tf_op jit(solution)/shard_map/all_to_all | solution.py:175
  355.0 29.9 %collective-permute-done.3 = bf16[360,1440]{1,0:T(8,128)(2,1)} collective-permute-done((bf16[360,1440]{1,0:T(8,128)(2,1)S(1)}, bf16[360,1440]{1,0:T(8,128)(2,1)}, u32[]{:S(2)}, u32[]{:S(2)}) %collective-permute-start.3) | collective-permute-done | bytes 1036832 | tf_op jit(solution)/shard_map/ppermute | solution.py:10
  384.9 4.1 fusion.3
  389.0 19.6 %collective-permute-done.2 = bf16[1440,360]{1,0:T(8,128)(2,1)} collective-permute-done((bf16[1440,360]{1,0:T(8,128)(2,1)S(1)}, bf16[1440,360]{1,0:T(8,128)(2,1)}, u32[]{:S(2)}, u32[]{:S(2)}) %collective-permute-start.2) | collective-permute-done | bytes 1036832 | tf_op jit(solution)/shard_map/ppermute | solution.py:10
  408.6 3.7 fusion.2
  412.7 3.0 gather_fusion.2
  415.7 2.9 reshape.323
  418.6 3.1 multiply_reduce_fusion
  422.7 1.6 reshape.322
  424.4 2.1 gather_fusion.5
  426.9 2.1 reduce_sum.55
  (107 shorter events, 18.4 us)
Async XLA Ops:
  7.2 4.9 %copy-start.13 = (s32[4,128]{1,0:T(4,128)S(1)}, s32[4,128]{1,0:T(4,128)}, u32[]{:S(2)}) copy-start(s32[4,128]{1,0:T(4,128)} %constant.140.clone.1) | copy-start | bytes 6148
  7.2 5.0 %copy-start.14 = (s32[128,4]{0,1:T(4,128)S(1)}, s32[128,4]{0,1:T(4,128)}, u32[]{:S(2)}) copy-start(s32[128,4]{0,1:T(4,128)} %param.11) | copy-start | bytes 6148
  7.2 82.8 %all-gather.3.cloned.1.call-start = ((), (), s32[]{:S(2)}) async-start(), calls=%async_computation.6 | async-start | bytes 4423680 | tf_op jit(solution)/shard_map/all_gather | solution.py:99
  8.7 4.0 copy-start.16
  8.7 8.2 %copy-start.11 = (bf16[128,1440]{0,1:T(8,128)(2,1)S(1)}, bf16[128,1440]{0,1:T(8,128)(2,1)}, u32[]{:S(2)}) copy-start(bf16[128,1440]{0,1:T(8,128)(2,1)} %param.10) | copy-start | bytes 1105924
  51.2 1.3 copy-start.15
  52.4 2.9 copy-start.12
  52.4 148.5 %all-gather.5.cloned.1.call-start = ((), (), s32[]{:S(2)}) async-start(), calls=%async_computation.8 | async-start | bytes 4423680 | tf_op jit(solution)/shard_map/all_gather | solution.py:125
  52.6 2.6 copy-start.9
  86.8 182.4 %reduce-scatter.3.cloned.1.call-start = ((), (), s32[]{:S(2)}) async-start(), calls=%async_computation.7 | async-start | bytes 9830400 | tf_op jit(solution)/shard_map/reduce_scatter | solution.py:115
  87.0 74.2 %collective-permute-start = (bf16[1,1440,360]{2,1,0:T(8,128)(2,1)}, bf16[1,1440,360]{2,1,0:T(8,128)(2,1)}, u32[]{:S(2)}, u32[]{:S(2)}) collective-permute-start(bf16[1,1440,360]{2,1,0:T(8,128)(2,1)} %param.15), channel_id=1, source_target_pairs={{0,16},{4,20},{8,24},{12,28},{16,0},{20,4},{24,8},{28,12},{1,17},{... | collective-permute-start | bytes 3110408 | tf_op jit(solution)/shard_map/ppermute | solution.py:10
  88.1 96.3 %collective-permute-start.1 = (bf16[1,360,1440]{2,1,0:T(8,128)(2,1)}, bf16[1,360,1440]{2,1,0:T(8,128)(2,1)}, u32[]{:S(2)}, u32[]{:S(2)}) collective-permute-start(bf16[1,360,1440]{2,1,0:T(8,128)(2,1)} %param.16), channel_id=1, source_target_pairs={{0,16},{4,20},{8,24},{12,28},{16,0},{20,4},{24,8},{28,12},{1,17},{... | collective-permute-start | bytes 3110408 | tf_op jit(solution)/shard_map/ppermute | solution.py:10
  90.0 1.7 slice-start
  94.4 1.4 slice-start.1
  97.0 67.0 %copy-start = (bf16[384,1440]{1,0:T(8,128)(2,1)}, bf16[384,1440]{1,0:T(8,128)(2,1)S(1)}, u32[]{:S(2)}) copy-start(bf16[384,1440]{1,0:T(8,128)(2,1)S(1)} %reshape.318) | copy-start | bytes 3317764
  186.4 1.7 copy-start.4
  200.7 140.4 %reduce-scatter.5.cloned.1.call-start = ((), (), s32[]{:S(2)}) async-start(), calls=%async_computation.9 | async-start | bytes 9830400 | tf_op jit(solution)/shard_map/reduce_scatter | solution.py:143
  200.9 1.7 slice-start.2
  205.4 1.6 slice-start.3
  208.3 3.2 copy-start.2
  211.6 0.7 copy-start.7
  214.7 1.8 copy-start.6
  214.7 2.1 copy-start.17
  271.7 5.7 %copy-start.3 = (bf16[384,1440]{1,0:T(8,128)(2,1)S(1)}, bf16[384,1440]{1,0:T(8,128)(2,1)}, u32[]{:S(2)}) copy-start(bf16[384,1440]{1,0:T(8,128)(2,1)} %copy-done.2) | copy-start | bytes 3317764
  271.7 78.8 %all-to-all-start.1 = ((bf16[8,36,1440]{2,1,0:T(8,128)(2,1)}), bf16[8,36,1440]{2,1,0:T(8,128)(2,1)S(1)}, u32[]{:S(2)}, u32[]{:S(2)}) async-start(bf16[8,36,1440]{2,1,0:T(8,128)(2,1)} %convert_element_type.79), calls=%async_computation.2 | async-start | bytes 1966080 | tf_op jit(solution)/shard_map/all_to_all | solution.py:123
  277.4 3.7 copy-start.1
  277.4 3.7 copy-start.8
  278.2 106.7 %collective-permute-start.3 = (bf16[360,1440]{1,0:T(8,128)(2,1)S(1)}, bf16[360,1440]{1,0:T(8,128)(2,1)}, u32[]{:S(2)}, u32[]{:S(2)}) collective-permute-start(bf16[360,1440]{1,0:T(8,128)(2,1)S(1)} %convolution_convert_fusion.1), channel_id=1, source_target_pairs={{0,16},{4,20},{8,24},{12,28},{16,0},{20,4},{24,8},{28,12},{1,17},{... | collective-permute-start | bytes 3110408 | tf_op jit(solution)/shard_map/ppermute | solution.py:10
  282.0 126.6 %collective-permute-start.2 = (bf16[1440,360]{1,0:T(8,128)(2,1)S(1)}, bf16[1440,360]{1,0:T(8,128)(2,1)}, u32[]{:S(2)}, u32[]{:S(2)}) collective-permute-start(bf16[1440,360]{1,0:T(8,128)(2,1)S(1)} %convolution_convert_fusion), channel_id=1, source_target_pairs={{0,16},{4,20},{8,24},{12,28},{16,0},{20,4},{24,8},{28,12},{1,17},{... | collective-permute-start | bytes 3110408 | tf_op jit(solution)/shard_map/ppermute | solution.py:10
  350.5 72.2 %all-to-all-start.3 = ((bf16[8,36,1440]{2,1,0:T(8,128)(2,1)}), bf16[8,36,1440]{2,1,0:T(8,128)(2,1)}, u32[]{:S(2)}, u32[]{:S(2)}) async-start(bf16[8,36,1440]{2,1,0:T(8,128)(2,1)} %convert_element_type.89), calls=%async_computation.5 | async-start | bytes 1966080 | tf_op jit(solution)/shard_map/all_to_all | solution.py:175
  355.0 53.6 %copy-start.5 = (bf16[32,24,1440]{2,1,0:T(8,128)(2,1)S(1)}, bf16[32,24,1440]{2,1,0:T(8,128)(2,1)}, u32[]{:S(2)}) copy-start(bf16[32,24,1440]{2,1,0:T(8,128)(2,1)} %copy.85) | copy-start | bytes 6635524
  355.0 53.6 %copy-start.10 = (bf16[768,360]{0,1:T(8,128)(2,1)S(1)}, bf16[768,360]{0,1:T(8,128)(2,1)}, u32[]{:S(2)}) copy-start(bf16[768,360]{0,1:T(8,128)(2,1)} %fusion) | copy-start | bytes 1658884
Sparse Core Ops, SparseCore 0:
  52.5 29.6 all-gather.2
  86.9 29.6 all-gather.4
  200.8 68.3 reduce-scatter.2
  271.5 69.5 reduce-scatter.4
where the time goes:
time: 443 us; the launch traced here: 437 us
  waiting for transfers between devices  238 us (54%)
  blocking collectives  59.1 us (13%)
  local copies, waits for them, and re-layouts  52.8 us (12%)
  matrix products  32.6 us (7%)
  other arithmetic  21.5 us (5%)
  starting transfers between devices  17.3 us (4%)
  between operations  15.4 us (3%)
    ppermute x4, waiting for transfers between devices, shifted(): return lax.ppermute(value, axis, pairs)  134 us
    reduce_scatter x1, waiting for transfers between devices, on_device(): lax.psum_scatter(slot_products(pre_all, w_first, copy_first, contract_las...  58.4 us
    reduce_scatter x1, waiting for transfers between devices, on_device(): lax.psum_scatter(slot_products(act_all, w_second, copy_second, contract_p...  39.4 us
    all_to_all x1, blocking collectives, on_device(): lax.all_to_all(sent_rows, 'expert', split_axis=0, concat_axis=0, tiled=True)  31.5 us
    all_to_all x1, blocking collectives, on_device(): lax.all_to_all(grad_rows, 'expert', split_axis=0, concat_axis=0, tiled=True)  27.5 us
  transfers between devices with their start and end apart: 10, of which 7 were waited for; matrix products, arithmetic and copies ran while one was open for 18% of the time, Pallas kernels for 0%

commit v1 on v0

v1 whole, which is shorter than its diff:
```python
import jax
import jax.numpy as jnp
from jax import lax
from jax.sharding import PartitionSpec as P

F32 = jnp.float32
BF16 = jnp.bfloat16


def activate(values):
    return values * jax.nn.sigmoid(1.702 * values)


def derivative(values):
    s = jax.nn.sigmoid(1.702 * values)
    return s + 1.702 * values * s * (1.0 - s)


def dot(a, b, dims):
    return lax.dot_general(a, b, (dims, ((), ())), preferred_element_type=F32)


def tables(routes, gate_fixed, live_count, plan, experts, capacity, spare):
    tokens = routes.shape[0]
    width = capacity + spare
    ids = jnp.arange(experts, dtype=jnp.int32)
    live = (jnp.arange(tokens, dtype=jnp.int32) < live_count)[:, None]
    same = routes[:, :, None] == ids[None, None, :]
    member = jnp.any(same, axis=1) & live
    gate = jnp.sum(jnp.where(same, gate_fixed[:, :, None], 0), axis=1)
    lower = (
        jnp.arange(tokens)[:, None] > jnp.arange(tokens)[None, :]
    ).astype(BF16)
    position = dot(lower, member.astype(BF16), ((1,), (0,))).astype(jnp.int32)
    hot = jnp.any(plan[:, None] == ids[None, :], axis=0)
    limit = capacity + spare * hot.astype(jnp.int32)
    position = jnp.where(member & (position < limit[None, :]), position, -1)
    slot = jnp.arange(width, dtype=jnp.int32)
    chosen = position[:, :, None] == slot[None, None, :]
    gates = jnp.where(chosen, gate[:, :, None], 0)
    chosen = chosen.reshape(tokens, experts * width)
    gates = gates.reshape(tokens, experts * width)
    return chosen.astype(BF16), gates


def on_device(tokens, routes, gate_fixed, counts, replica_plan, weight_in, weight_out, cotangent):
    token_count, features = tokens.shape
    top_count = routes.shape[1]
    groups = lax.axis_size("expert")
    experts = groups * weight_in.shape[0]
    capacity = 3 * token_count * top_count // (8 * experts)
    spare = capacity // 2
    width = capacity + spare
    chosen, gates = tables(
        routes, gate_fixed, counts[0], replica_plan, experts, capacity, spare
    )
    high = (gates // 256).astype(BF16)
    low = (gates % 256).astype(BF16)
    slot_scale = jnp.sum(gates, axis=0).astype(F32) / 65536.0
    sent = dot(chosen, tokens, ((0,), (0,))).astype(BF16).reshape(experts, width, features)
    grads = (dot(chosen, cotangent, ((0,), (0,))) * slot_scale[:, None]).astype(BF16)
    grads = grads.reshape(experts, width, features)
    w1 = weight_in[0]
    w2 = weight_out[0]

    def exchange(value):
        return lax.all_to_all(value, "expert", split_axis=0, concat_axis=0, tiled=True)

    rows = lax.all_gather(exchange(sent), "dp", axis=0, tiled=True).reshape(-1, features)
    grad = lax.all_gather(exchange(grads), "dp", axis=0, tiled=True).reshape(-1, features)
    pre = dot(rows, w1, ((1,), (0,)))
    act = activate(pre).astype(BF16)
    out = dot(act, w2, ((1,), (0,))).astype(BF16)
    out = out.reshape(-1, width, features)
    out = lax.psum_scatter(out, "dp", scatter_dimension=0, tiled=True)
    returned = exchange(out.astype(BF16)).reshape(-1, features)
    act_grad = dot(grad, w2, ((1,), (1,)))
    pre_grad = (act_grad * derivative(pre)).astype(BF16)
    dx = dot(pre_grad, w1, ((1,), (1,))).astype(BF16).reshape(-1, width, features)
    dx = lax.psum_scatter(dx, "dp", scatter_dimension=0, tiled=True)
    returned_dx = exchange(dx.astype(BF16)).reshape(-1, features)
    w2_grad = dot(act, grad, ((0,), (0,))).astype(BF16)[None]
    w1_grad = dot(rows, pre_grad, ((0,), (0,))).astype(BF16)[None]
    layer = dot(high, returned, ((1,), (0,))) * (1.0 / 256.0) + dot(
        low, returned, ((1,), (0,))
    ) * (1.0 / 65536.0)
    dx_sum = dot(chosen, returned_dx, ((1,), (0,)))
    return (layer.astype(BF16), dx_sum.astype(BF16), w1_grad, w2_grad)


def solution(mesh):
    both = P(("expert", "dp"), None)
    return jax.shard_map(
        on_device,
        mesh=mesh,
        in_specs=(
            both,
            both,
            both,
            P(("expert", "dp")),
            P(),
            P("expert", None, "dp"),
            P("expert", "dp", None),
            both,
        ),
        out_specs=(both, both, P("expert", None, "dp"), P("expert", "dp", None)),
        check_vma=False,
    )
```

time: 443 us -> 237 us (0.53); the launches traced: 437 us -> 235 us
  waiting for transfers between devices: 238 us -> 67.3 us
  other arithmetic: 21.5 us -> 1.77 us
  starting transfers between devices: 17.3 us -> 11.4 us
    ppermute x4 -> x0, waiting for transfers between devices: 134 us -> none  [shifted(): return lax.ppermute(value, axis, pairs)]
    reduce_scatter x2, waiting for transfers between devices: 97.9 us -> 52.8 us  [the longest x1 39.8 us: on_device(): dx = lax.psum_scatter(dx, 'dp', scatter_dimension=0, tiled=True)]
    reshape x5 -> x6, local copies, waits for them, and re-layouts: 3.27 us -> 25.3 us  [the longest x1 6.39 us: on_device(): lax.all_gather(exchange(grads), 'dp', axis=0, tiled=True)]
    gather x8 -> x0, local copies, waits for them, and re-layouts: 16 us -> none  [the longest x3 5.52 us: gather_back(): return padded[slot_index].astype(jnp.float32)]
    slice x12 -> x0, local copies, waits for them, and re-layouts: 13.2 us -> none  [the longest x3 4.46 us: on_device(): own_grad = all_grad[:, :capacity].reshape(-1, features)]
    all_gather x0 -> x2, local copies, waits for them, and re-layouts: none -> 11.6 us  [the longest x1 5.83 us: on_device(): lax.all_gather(exchange(grads), 'dp', axis=0, tiled=True)]
    concatenate x2 -> x0, other arithmetic: 8.27 us -> none  [slot_products(): jnp.concatenate([own_term.reshape(amount, capacity, -1), copy_term.reshap...]
    all_to_all x2, waiting for transfers between devices: 6.8 us -> 14.3 us  [exchange(): lax.all_to_all(value, 'expert', split_axis=0, concat_axis=0, tiled=True)]
  transfers between devices with their start and end apart: 10 -> 6, of which waited for: 7 -> 4; matrix products, arithmetic and copies ran while one was open for 18% -> 32% of each run, Pallas kernels for 0% -> 0%
where the time goes in v1:
time: 237 us; the launch traced here: 235 us
  waiting for transfers between devices  67.3 us (28%)
  blocking collectives  59.1 us (25%)
  local copies, waits for them, and re-layouts  52.3 us (22%)
  matrix products  29 us (12%)
  between operations  14.7 us (6%)
  starting transfers between devices  11.4 us (5%)
    all_to_all x2, blocking collectives, exchange(): lax.all_to_all(value, 'expert', split_axis=0, concat_axis=0, tiled=True)  59.1 us
    reduce_scatter x1, waiting for transfers between devices, on_device(): dx = lax.psum_scatter(dx, 'dp', scatter_dimension=0, tiled=True)  39.8 us
    dot_general x12, matrix products, dot(): return lax.dot_general(a, b, (dims, ((), ())), preferred_element_type=F32)  29 us
    all_to_all x2, waiting for transfers between devices, exchange(): lax.all_to_all(value, 'expert', split_axis=0, concat_axis=0, tiled=True)  14.3 us
    reduce_scatter x1, waiting for transfers between devices, on_device(): out = lax.psum_scatter(out, 'dp', scatter_dimension=0, tiled=True)  12.9 us
    all_to_all x2, starting transfers between devices, exchange(): lax.all_to_all(value, 'expert', split_axis=0, concat_axis=0, tiled=True)  11 us
    reshape x1, local copies, waits for them, and re-layouts, on_device(): lax.all_gather(exchange(grads), 'dp', axis=0, tiled=True)  6.39 us
    reshape x1, local copies, waits for them, and re-layouts, on_device(): lax.all_gather(exchange(sent), 'dp', axis=0, tiled=True)  6.17 us
  transfers between devices with their start and end apart: 6, of which 4 were waited for; matrix products, arithmetic and copies ran while one was open for 32% of the time, Pallas kernels for 0%

profile of v1, /device:TPU:0, one launch (start us, length us, event | category | flops | bytes accessed | tf_op | source)
XLA Modules:
  0.0 235.4 jit_solution(7886613969575222244)
XLA Ops:
  7.2 0.0 all-gather.3.cloned.1.call-start
  8.0 0.7 fusion.39
  8.7 0.7 fusion.37
  9.4 0.1 eq.67
  9.5 0.1 and_select_fusion
  9.6 0.1 eq.62
  9.7 0.1 broadcast_compare_fusion
  9.8 1.4 convolution_convert_fusion.4
  11.2 0.2 reshape.76
  11.4 31.5 %all_to_all.20 = bf16[8,36,1440]{2,1,0:T(8,128)(2,1)S(1)} all-to-all(bf16[8,36,1440]{2,1,0:T(8,128)(2,1)S(1)} %reshape.76), channel_id=1, replica_groups=mesh['expert'=8,'dp'=4] {'expert'}, dimensions={0} | all-to-all | bytes 1658880 | tf_op jit(solution)/shard_map/all_to_all | solution.py:67
  43.0 1.2 copy.28
  44.2 0.0 all-gather.3.cloned.1.call-update
  44.2 0.0 all-gather.5.cloned.1.call-start
  44.3 0.2 select_reduce_fusion
  44.5 0.1 div.31
  44.6 0.4 fusion.1
  45.0 0.2 reshape.79
  45.2 27.5 %all_to_all.21 = bf16[8,36,1440]{2,1,0:T(8,128)(2,1)S(1)} all-to-all(bf16[8,36,1440]{2,1,0:T(8,128)(2,1)S(1)} %reshape.79), channel_id=1, replica_groups=mesh['expert'=8,'dp'=4] {'expert'}, dimensions={0} | all-to-all | bytes 1658880 | tf_op jit(solution)/shard_map/all_to_all | solution.py:67
  72.8 1.2 copy.31
  73.9 0.0 all-gather.5.cloned.1.call-update
  73.9 0.0 reduce-scatter.3.cloned.1.call-start
  74.0 0.0 all-gather.3.cloned.1.call-done
  74.0 5.8 %copy.29 = bf16[32,36,1440]{2,1,0:T(8,128)(2,1)} copy(bf16[32,36,1440]{2,0,1:T(8,128)(2,1)} %all-gather.3.cloned.1.call-done) | data formatting | bytes 6635520 | tf_op jit(solution)/shard_map/all_gather | solution.py:69
  79.8 6.2 %reshape.77 = bf16[1152,1440]{1,0:T(8,128)(2,1)} reshape(bf16[32,36,1440]{2,1,0:T(8,128)(2,1)} %copy.29) | data formatting | bytes 6635520 | tf_op jit(solution)/shard_map/reshape | solution.py:69
  86.0 3.7 %fusion.12 = f32[1152,360]{0,1:T(8,128)S(1)} fusion(bf16[1152,1440]{1,0:T(8,128)(2,1)} %reshape.77, bf16[1,1440,360]{2,1,0:T(8,128)(2,1)S(1)} %copy-done.5), kind=kOutput, calls=%fused_computation.25 | convolution fusion | flops 1194393600 | bytes 6013440 | tf_op jit(solution)/shard_map/dot_general | solution.py:20
  89.7 1.2 copy-done.7
  90.9 3.8 %convolution_convert_fusion.1 = bf16[1152,1440]{0,1:T(8,128)(2,1)} fusion(bf16[1,360,1440]{2,1,0:T(8,128)(2,1)S(1)} %copy-done, f32[1152,360]{0,1:T(8,128)S(1)} %fusion.12), kind=kOutput, calls=%fused_computation.1 | convolution fusion | flops 1198540800 | bytes 6013440 | tf_op jit(solution)/shard_map/dot_general | solution.py:20
  94.7 5.7 %copy.30 = bf16[1152,1440]{1,0:T(8,128)(2,1)} copy(bf16[1152,1440]{0,1:T(8,128)(2,1)} %convolution_convert_fusion.1) | data formatting | bytes 6635520 | tf_op jit(solution)/shard_map/convert_element_type | solution.py:73
  100.4 6.2 %reshape.78 = bf16[32,36,1440]{2,1,0:T(8,128)(2,1)} reshape(bf16[1152,1440]{1,0:T(8,128)(2,1)} %copy.30) | data formatting | bytes 6635520 | tf_op jit(solution)/shard_map/reshape | solution.py:74
  106.5 0.0 reduce-scatter.3.cloned.1.call-update
  106.6 0.2 reduce-scatter.5.cloned.1.call-start
  106.8 0.1 all-gather.5.cloned.1.call-done
  106.9 5.8 %copy.32 = bf16[32,36,1440]{2,1,0:T(8,128)(2,1)} copy(bf16[32,36,1440]{2,0,1:T(8,128)(2,1)} %all-gather.5.cloned.1.call-done) | data formatting | bytes 6635520 | tf_op jit(solution)/shard_map/all_gather | solution.py:70
  112.7 6.4 %reshape.80 = bf16[1152,1440]{1,0:T(8,128)(2,1)} reshape(bf16[32,36,1440]{2,1,0:T(8,128)(2,1)} %copy.32) | data formatting | bytes 6635520 | tf_op jit(solution)/shard_map/reshape | solution.py:70
  119.1 4.5 %fusion = bf16[1152,360]{0,1:T(8,128)(2,1)S(1)} fusion(bf16[1152,1440]{1,0:T(8,128)(2,1)} %reshape.80, f32[1152,360]{0,1:T(8,128)} %copy-done.7, bf16[1,360,1440]{2,1,0:T(8,128)(2,1)S(1)} %copy-done), kind=kOutput, calls=%fused_computation.5 | convolution fusion | flops 1198540800 | bytes 6842880 | tf_op jit(solution)/shard_map/dot_general | solution.py:20
  123.7 3.7 %convolution_convert_fusion = bf16[1152,1440]{0,1:T(8,128)(2,1)} fusion(bf16[1152,360]{0,1:T(8,128)(2,1)S(1)} %fusion, bf16[1,1440,360]{2,1,0:T(8,128)(2,1)S(1)} %copy-done.5), kind=kOutput, calls=%fused_computation | convolution fusion | flops 1196052480 | bytes 5184000 | tf_op jit(solution)/shard_map/dot_general | solution.py:20
  127.4 5.9 %copy.33 = bf16[1152,1440]{1,0:T(8,128)(2,1)} copy(bf16[1152,1440]{0,1:T(8,128)(2,1)} %convolution_convert_fusion) | data formatting | bytes 6635520 | tf_op jit(solution)/shard_map/convert_element_type | solution.py:79
  133.3 6.1 %reshape.81 = bf16[32,36,1440]{2,1,0:T(8,128)(2,1)} reshape(bf16[1152,1440]{1,0:T(8,128)(2,1)} %copy.33) | data formatting | bytes 6635520 | tf_op jit(solution)/shard_map/reshape | solution.py:79
  139.5 12.9 %reduce-scatter.3.cloned.1.call-done = bf16[8,36,1440]{2,1,0:T(8,128)(2,1)} async-done(((bf16[32,36,1440]{2,1,0:T(8,128)(2,1)}), bf16[8,36,1440]{2,1,0:T(8,128)(2,1)}) %reduce-scatter.3.cloned.1.call-update) | async-done | bytes 829456 | tf_op jit(solution)/shard_map/reduce_scatter | solution.py:75
  152.4 5.5 %all-to-all-start.1 = ((bf16[8,36,1440]{2,1,0:T(8,128)(2,1)}), bf16[8,36,1440]{2,1,0:T(8,128)(2,1)S(1)}, u32[]{:S(2)}, u32[]{:S(2)}) async-start(bf16[8,36,1440]{2,1,0:T(8,128)(2,1)} %reduce-scatter.3.cloned.1.call-done), calls=%async_computation.2 | async-start | bytes 1966080 | tf_op jit(solution)/shard_map/all_to_all | solution.py:67
  157.9 39.8 %reduce-scatter.5.cloned.1.call-done = bf16[8,36,1440]{2,1,0:T(8,128)(2,1)} async-done(((bf16[32,36,1440]{2,1,0:T(8,128)(2,1)}), bf16[8,36,1440]{2,1,0:T(8,128)(2,1)}) %reduce-scatter.5.cloned.1.call-update) | async-done | bytes 829456 | tf_op jit(solution)/shard_map/reduce_scatter | solution.py:80
  197.7 5.5 %all-to-all-start.3 = ((bf16[8,36,1440]{2,1,0:T(8,128)(2,1)}), bf16[8,36,1440]{2,1,0:T(8,128)(2,1)S(1)}, u32[]{:S(2)}, u32[]{:S(2)}) async-start(bf16[8,36,1440]{2,1,0:T(8,128)(2,1)} %reduce-scatter.5.cloned.1.call-done), calls=%async_computation.5 | async-start | bytes 1966080 | tf_op jit(solution)/shard_map/all_to_all | solution.py:67
  203.3 5.5 %fusion.2 = bf16[1,1440,360]{2,1,0:T(8,128)(2,1)} fusion(bf16[1152,1440]{1,0:T(8,128)(2,1)} %reshape.77, bf16[1152,360]{0,1:T(8,128)(2,1)} %copy-done.6), kind=kOutput, calls=%fused_computation.9 | convolution fusion | flops 1194912000 | bytes 5184000 | tf_op jit(solution)/shard_map/dot_general | solution.py:20
  208.7 2.6 %fusion.3 = bf16[1,360,1440]{2,1,0:T(8,128)(2,1)} fusion(bf16[1152,1440]{1,0:T(8,128)(2,1)S(1)} %copy-done.1, f32[1152,360]{0,1:T(8,128)S(1)} %copy-done.8), kind=kOutput, calls=%fused_computation.10 | convolution fusion | flops 1197400320 | bytes 6013440 | tf_op jit(solution)/shard_map/dot_general | solution.py:20
  211.4 0.6 fusion.6
  212.0 1.3 fusion.7
  213.3 14.3 %all-to-all-done.3 = bf16[8,36,1440]{2,1,0:T(8,128)(2,1)S(1)} async-done(((bf16[8,36,1440]{2,1,0:T(8,128)(2,1)}), bf16[8,36,1440]{2,1,0:T(8,128)(2,1)S(1)}, u32[]{:S(2)}, u32[]{:S(2)}) %all-to-all-start.3) | async-done | bytes 829472 | tf_op jit(solution)/shard_map/all_to_all | solution.py:67
  227.6 1.3 fusion.8
  (25 shorter events, 0.1 us)
Async XLA Ops:
  7.2 83.7 %copy-start = (bf16[1,360,1440]{2,1,0:T(8,128)(2,1)S(1)}, bf16[1,360,1440]{2,1,0:T(8,128)(2,1)}, u32[]{:S(2)}) copy-start(bf16[1,360,1440]{2,1,0:T(8,128)(2,1)} %param.14) | copy-start | bytes 3110404
  7.2 66.8 %all-gather.3.cloned.1.call-start = ((), (), s32[]{:S(2)}) async-start(), calls=%async_computation.6 | async-start | bytes 4423680 | tf_op jit(solution)/shard_map/all_gather | solution.py:69
  43.0 1.3 copy-start.3
  43.0 1.3 copy-start.4
  43.0 1.6 copy-start.2
  44.2 62.7 %all-gather.5.cloned.1.call-start = ((), (), s32[]{:S(2)}) async-start(), calls=%async_computation.8 | async-start | bytes 4423680 | tf_op jit(solution)/shard_map/all_gather | solution.py:70
  73.9 78.4 %reduce-scatter.3.cloned.1.call-start = ((), (), s32[]{:S(2)}) async-start(), calls=%async_computation.7 | async-start | bytes 4915200 | tf_op jit(solution)/shard_map/reduce_scatter | solution.py:75
  79.8 6.2 %copy-start.5 = (bf16[1,1440,360]{2,1,0:T(8,128)(2,1)S(1)}, bf16[1,1440,360]{2,1,0:T(8,128)(2,1)}, u32[]{:S(2)}) copy-start(bf16[1,1440,360]{2,1,0:T(8,128)(2,1)} %param.13) | copy-start | bytes 3110404
  89.7 1.2 copy-start.7
  106.6 91.2 %reduce-scatter.5.cloned.1.call-start = ((), (), s32[]{:S(2)}) async-start(), calls=%async_computation.9 | async-start | bytes 4915200 | tf_op jit(solution)/shard_map/reduce_scatter | solution.py:80
  123.6 3.8 %copy-start.6 = (bf16[1152,360]{0,1:T(8,128)(2,1)}, bf16[1152,360]{0,1:T(8,128)(2,1)S(1)}, u32[]{:S(2)}) copy-start(bf16[1152,360]{0,1:T(8,128)(2,1)S(1)} %fusion) | copy-start | bytes 2488324
  152.4 45.4 %all-to-all-start.1 = ((bf16[8,36,1440]{2,1,0:T(8,128)(2,1)}), bf16[8,36,1440]{2,1,0:T(8,128)(2,1)S(1)}, u32[]{:S(2)}, u32[]{:S(2)}) async-start(bf16[8,36,1440]{2,1,0:T(8,128)(2,1)} %reduce-scatter.3.cloned.1.call-done), calls=%async_computation.2 | async-start | bytes 1966080 | tf_op jit(solution)/shard_map/all_to_all | solution.py:67
  197.7 29.8 %all-to-all-start.3 = ((bf16[8,36,1440]{2,1,0:T(8,128)(2,1)}), bf16[8,36,1440]{2,1,0:T(8,128)(2,1)S(1)}, u32[]{:S(2)}, u32[]{:S(2)}) async-start(bf16[8,36,1440]{2,1,0:T(8,128)(2,1)} %reduce-scatter.5.cloned.1.call-done), calls=%async_computation.5 | async-start | bytes 1966080 | tf_op jit(solution)/shard_map/all_to_all | solution.py:67
  203.3 5.5 %copy-start.1 = (bf16[1152,1440]{1,0:T(8,128)(2,1)S(1)}, bf16[1152,1440]{1,0:T(8,128)(2,1)}, u32[]{:S(2)}) copy-start(bf16[1152,1440]{1,0:T(8,128)(2,1)} %reshape.80) | copy-start | bytes 9953284
  203.3 5.5 %copy-start.8 = (f32[1152,360]{0,1:T(8,128)S(1)}, f32[1152,360]{0,1:T(8,128)}, u32[]{:S(2)}) copy-start(f32[1152,360]{0,1:T(8,128)} %copy-done.7) | copy-start | bytes 4976644
Sparse Core Ops, SparseCore 0:
  44.3 29.6 all-gather.2
  76.1 30.7 all-gather.4
  109.5 42.8 reduce-scatter.2
  154.8 42.9 reduce-scatter.4

commit v2 on v1

v2 whole, which is shorter than its diff:
```python
import jax
import jax.numpy as jnp
from jax import lax
from jax.experimental import pallas as pl
from jax.experimental.pallas import tpu as pltpu
from jax.sharding import PartitionSpec as P

F32 = jnp.float32
BF16 = jnp.bfloat16
MESH = pl.DeviceIdType.MESH


def activate(values):
    return values * jax.nn.sigmoid(1.702 * values)


def derivative(values):
    s = jax.nn.sigmoid(1.702 * values)
    return s + 1.702 * values * s * (1.0 - s)


def dot(a, b, dims):
    return lax.dot_general(a, b, (dims, ((), ())), preferred_element_type=F32)


def tables(routes, gate_fixed, live_count, plan, experts, capacity, spare, width):
    tokens = routes.shape[0]
    ids = jnp.arange(experts, dtype=jnp.int32)
    live = (jnp.arange(tokens, dtype=jnp.int32) < live_count)[:, None]
    same = routes[:, :, None] == ids[None, None, :]
    member = jnp.any(same, axis=1) & live
    gate = jnp.sum(jnp.where(same, gate_fixed[:, :, None], 0), axis=1)
    lower = (
        jnp.arange(tokens)[:, None] > jnp.arange(tokens)[None, :]
    ).astype(BF16)
    position = dot(lower, member.astype(BF16), ((1,), (0,))).astype(jnp.int32)
    hot = jnp.any(plan[:, None] == ids[None, :], axis=0)
    limit = capacity + spare * hot.astype(jnp.int32)
    position = jnp.where(member & (position < limit[None, :]), position, -1)
    slot = jnp.arange(width, dtype=jnp.int32)
    chosen = position[:, :, None] == slot[None, None, :]
    gates = jnp.where(chosen, gate[:, :, None], 0)
    chosen = chosen.reshape(tokens, experts * width)
    gates = gates.reshape(tokens, experts * width)
    return chosen.astype(BF16), gates


def places(experts):
    e = lax.axis_index("expert")
    d = lax.axis_index("dp")
    core = d % 2
    partner = d + 1 - 2 * core
    cross = (d + 2) % 4
    return e, d, core, partner, cross


def remote(src, dst, send, recv, target):
    return pltpu.make_async_remote_copy(
        src_ref=src,
        dst_ref=dst,
        send_sem=send,
        recv_sem=recv,
        device_id=target,
        device_id_type=MESH,
    )


def greet(experts, e, d, partner, cross):
    barrier = pltpu.get_barrier_semaphore()
    pl.semaphore_signal(barrier, inc=1, device_id=(e, partner), device_id_type=MESH)
    pl.semaphore_signal(barrier, inc=1, device_id=(e, cross), device_id_type=MESH)

    @pl.loop(1, experts)
    def _(k):
        pl.semaphore_signal(
            barrier, inc=1, device_id=((e + k) % experts, d), device_id_type=MESH
        )

    pl.semaphore_wait(barrier, experts + 1)


def inbound_kernel(
    experts, tok, grad, w1, w2, rows, grads, w1x, w2x,
    a_send, a_recv, c_send, c_recv, w_send, w_recv, own_sem,
):
    e, d, core, partner, cross = places(experts)
    greet(experts, e, d, partner, cross)
    sides = ((tok, rows), (grad, grads))
    weights = [
        remote(src, dst, w_send.at[i], w_recv.at[i], (e, cross))
        for i, (src, dst) in enumerate(((w1, w1x), (w2, w2x)))
    ]
    for copy in weights:
        copy.start()

    def across(j, k):
        src, dst = sides[j]
        target = (e + k) % experts
        return remote(
            src.at[target], dst.at[core, e], a_send.at[j, k], a_recv.at[j, k], (target, d)
        )

    def along(j, k):
        dst = sides[j][1]
        source = (e + experts - k) % experts
        return remote(
            dst.at[core, source],
            dst.at[core, source],
            c_send.at[j, k],
            c_recv.at[j, k],
            (e, partner),
        )

    owns = []
    for j in range(2):
        @pl.loop(1, experts)
        def _(k):
            across(j, k).start()

        own = pltpu.make_async_copy(sides[j][0].at[e], sides[j][1].at[core, e], own_sem.at[j])
        own.start()
        owns.append(own)
    for j in range(2):
        owns[j].wait()
        along(j, 0).start()

        @pl.loop(1, experts)
        def _(k):
            across(j, k).wait_recv()
            along(j, k).start()

    for j in range(2):
        @pl.loop(1, experts)
        def _(k):
            across(j, k).wait_send()

        @pl.loop(0, experts)
        def _(k):
            copy = along(j, k)
            copy.wait_send()
            copy.wait_recv()

    for copy in weights:
        copy.wait()


def outbound_kernel(
    experts, out, dx, g1, g2, ret, ret_dx, g1x, g2x,
    part, summed, a_send, a_recv, c_send, c_recv, w_send, w_recv,
):
    e, d, core, partner, cross = places(experts)
    greet(experts, e, d, partner, cross)
    sides = ((out, ret), (dx, ret_dx))

    def along(j, k):
        target = (e + k) % experts
        return remote(
            sides[j][0].at[1 - core, target],
            part.at[j, target],
            c_send.at[j, k],
            c_recv.at[j, k],
            (e, partner),
        )

    def across(j, k):
        target = (e + k) % experts
        return remote(
            summed.at[j, target],
            sides[j][1].at[e],
            a_send.at[j, k],
            a_recv.at[j, k],
            (target, d),
        )

    for j in range(2):
        @pl.loop(1, experts + 1)
        def _(k):
            along(j, k % experts).start()

    weights = [
        remote(src, dst, w_send.at[i], w_recv.at[i], (e, cross))
        for i, (src, dst) in enumerate(((g1, g1x), (g2, g2x)))
    ]
    for copy in weights:
        copy.start()

    for j in range(2):
        @pl.loop(1, experts)
        def _(k):
            along(j, k).wait_recv()
            target = (e + k) % experts
            total = sides[j][0][core, target].astype(F32) + part[j, target].astype(F32)
            summed[j, target] = total.astype(BF16)
            across(j, k).start()

        along(j, 0).wait_recv()
        total = sides[j][0][core, e].astype(F32) + part[j, e].astype(F32)
        sides[j][1][e] = total.astype(BF16)

    for j in range(2):
        @pl.loop(0, experts)
        def _(k):
            along(j, k).wait_send()

        @pl.loop(1, experts)
        def _(k):
            copy = across(j, k)
            copy.wait_send()
            copy.wait_recv()

    for copy in weights:
        copy.wait()


def inbound(experts, sent, grads, w1, w2):
    vm = pl.BlockSpec(memory_space=pltpu.VMEM)
    anywhere = pl.BlockSpec(memory_space=pl.ANY)
    dma = pltpu.SemaphoreType.DMA
    rows = jax.ShapeDtypeStruct((2,) + sent.shape, BF16)
    return pl.pallas_call(
        lambda *refs: inbound_kernel(experts, *refs),
        out_shape=(
            rows,
            rows,
            jax.ShapeDtypeStruct(w1.shape, BF16),
            jax.ShapeDtypeStruct(w2.shape, BF16),
        ),
        in_specs=[vm, vm, anywhere, anywhere],
        out_specs=(vm, vm, anywhere, anywhere),
        scratch_shapes=[dma((2, experts))] * 4 + [dma((2,))] * 3,
        compiler_params=pltpu.CompilerParams(collective_id=0, has_side_effects=True),
        name="inbound",
    )(sent, grads, w1, w2)


def outbound(experts, out, dx, g1, g2):
    vm = pl.BlockSpec(memory_space=pltpu.VMEM)
    anywhere = pl.BlockSpec(memory_space=pl.ANY)
    dma = pltpu.SemaphoreType.DMA
    rows = jax.ShapeDtypeStruct(out.shape[1:], BF16)
    return pl.pallas_call(
        lambda *refs: outbound_kernel(experts, *refs),
        out_shape=(
            rows,
            rows,
            jax.ShapeDtypeStruct(g1.shape, BF16),
            jax.ShapeDtypeStruct(g2.shape, BF16),
        ),
        in_specs=[vm, vm, anywhere, anywhere],
        out_specs=(vm, vm, anywhere, anywhere),
        scratch_shapes=[pltpu.VMEM((2,) + out.shape[1:], BF16)] * 2
        + [dma((2, experts))] * 4
        + [dma((2,))] * 2,
        compiler_params=pltpu.CompilerParams(collective_id=1, has_side_effects=True),
        name="outbound",
    )(out, dx, g1, g2)


def on_device(tokens, routes, gate_fixed, counts, replica_plan, weight_in, weight_out, cotangent):
    token_count, features = tokens.shape
    top_count = routes.shape[1]
    experts = lax.axis_size("expert") * weight_in.shape[0]
    capacity = 3 * token_count * top_count // (8 * experts)
    spare = capacity // 2
    width = -(-(capacity + spare) // 8) * 8
    chosen, gates = tables(
        routes, gate_fixed, counts[0], replica_plan, experts, capacity, spare, width
    )
    high = (gates // 256).astype(BF16)
    low = (gates % 256).astype(BF16)
    slot_scale = jnp.sum(gates, axis=0).astype(F32) / 65536.0
    sent = dot(chosen, tokens, ((0,), (0,))).astype(BF16).reshape(experts, width, features)
    grads = (dot(chosen, cotangent, ((0,), (0,))) * slot_scale[:, None]).astype(BF16)
    grads = grads.reshape(experts, width, features)
    w1 = weight_in[0]
    w2 = weight_out[0]
    rows, grad, w1x, w2x = inbound(experts, sent, grads, w1, w2)
    blocks = rows.shape
    rows = rows.reshape(-1, features)
    grad = grad.reshape(-1, features)

    def forward(first, second):
        pre = dot(rows, first, ((1,), (0,)))
        act = activate(pre).astype(BF16)
        act_grad = dot(grad, second, ((1,), (1,)))
        pre_grad = (act_grad * derivative(pre)).astype(BF16)
        g2 = dot(act, grad, ((0,), (0,)))
        g1 = dot(rows, pre_grad, ((0,), (0,)))
        return act, pre_grad, g1, g2

    act, pre_grad, g1, g2 = forward(w1, w2)
    act_x, pre_grad_x, g1_x, g2_x = forward(w1x, w2x)
    plain = ((1,), (0,))
    last = ((1,), (1,))
    out = (dot(act, w2, plain) + dot(act_x, w2x, plain)).astype(BF16)
    dx = (dot(pre_grad, w1, last) + dot(pre_grad_x, w1x, last)).astype(BF16)
    ret, ret_dx, g1_in, g2_in = outbound(
        experts, out.reshape(blocks), dx.reshape(blocks), g1_x.astype(BF16), g2_x.astype(BF16)
    )
    w1_grad = (g1 + g1_in.astype(F32)).astype(BF16)[None]
    w2_grad = (g2 + g2_in.astype(F32)).astype(BF16)[None]
    ret = ret.reshape(-1, features)
    ret_dx = ret_dx.reshape(-1, features)
    layer = dot(high, ret, plain) * (1.0 / 256.0) + dot(low, ret, plain) * (1.0 / 65536.0)
    dx_sum = dot(chosen, ret_dx, plain)
    return (layer.astype(BF16), dx_sum.astype(BF16), w1_grad, w2_grad)


def solution(mesh):
    both = P(("expert", "dp"), None)
    return jax.shard_map(
        on_device,
        mesh=mesh,
        in_specs=(
            both,
            both,
            both,
            P(("expert", "dp")),
            P(),
            P("expert", None, "dp"),
            P("expert", "dp", None),
            both,
        ),
        out_specs=(both, both, P("expert", None, "dp"), P("expert", "dp", None)),
        check_vma=False,
    )
```

time: 237 us -> 158 us (0.67)
  Pallas kernels: 0 us -> 113 us
  waiting for transfers between devices: 67.3 us -> 0 us
  blocking collectives: 59.1 us -> 0 us
  local copies, waits for them, and re-layouts: 52.3 us -> 7.84 us
  between operations: 14.7 us -> 1.56 us
  starting transfers between devices: 11.4 us -> 0 us
  matrix products: 29 us -> 32.3 us
    pallas_call x0 -> x2, Pallas kernels: none -> 113 us  [the longest x1 59.7 us: inbound(): pl.pallas_call(lambda *refs: inbound_kernel(experts, *refs), out_shape=(r...]
    all_to_all x2 -> x0, blocking collectives: 59.1 us -> none  [exchange(): lax.all_to_all(value, 'expert', split_axis=0, concat_axis=0, tiled=True)]
    reduce_scatter x2 -> x0, waiting for transfers between devices: 52.8 us -> none  [the longest x1 39.8 us: on_device(): dx = lax.psum_scatter(dx, 'dp', scatter_dimension=0, tiled=True)]
    reshape x6 -> x0, local copies, waits for them, and re-layouts: 25.3 us -> none  [the longest x1 6.39 us: on_device(): lax.all_gather(exchange(grads), 'dp', axis=0, tiled=True)]
    all_to_all x2 -> x0, waiting for transfers between devices: 14.3 us -> none  [exchange(): lax.all_to_all(value, 'expert', split_axis=0, concat_axis=0, tiled=True)]
    all_gather x2 -> x0, local copies, waits for them, and re-layouts: 11.6 us -> none  [the longest x1 5.83 us: on_device(): lax.all_gather(exchange(grads), 'dp', axis=0, tiled=True)]
    all_to_all x2 -> x0, starting transfers between devices: 11 us -> none  [exchange(): lax.all_to_all(value, 'expert', split_axis=0, concat_axis=0, tiled=True)]
    convert_element_type x2, local copies, waits for them, and re-layouts: 11.6 us -> 4.92 us  [the longest x1 2.46 us: on_device(): dx = (dot(pre_grad, w1, last) + dot(pre_grad_x, w1x, last)).astype(BF16)]
  transfers between devices with their start and end apart: 6 -> 0, of which waited for: 4 -> 0; matrix products, arithmetic and copies ran while one was open for 32% -> 0% of each run, Pallas kernels for 0% -> 0%
where the time goes in v2:
time: 158 us
  Pallas kernels  113 us (72%)
  matrix products  32.3 us (20%)
  local copies, waits for them, and re-layouts  7.84 us (5%)
  other arithmetic  2.55 us (2%)
    pallas_call x1, Pallas kernels, inbound(): pl.pallas_call(lambda *refs: inbound_kernel(experts, *refs), out_shape=(r...  59.7 us
    pallas_call x1, Pallas kernels, outbound(): pl.pallas_call(lambda *refs: outbound_kernel(experts, *refs), out_shape=(...  53.6 us
    dot_general x18, matrix products, dot(): return lax.dot_general(a, b, (dims, ((), ())), preferred_element_type=F32)  32.3 us

profile of v2, /device:TPU:0, one launch (start us, length us, event | category | flops | bytes accessed | tf_op | source)
XLA Modules:
  0.0 157.6 jit_solution(4017409466902508851)
XLA Ops:
  0.6 0.0 copy-start
  0.7 0.1 eq.67
  0.7 0.7 fusion.37
  1.5 0.7 fusion.39
  2.9 0.1 and_select_fusion
  3.0 0.2 bitcast_compare_fusion
  3.1 0.0 copy-done
  3.2 1.4 convolution_convert_fusion.2
  4.5 0.7 select_reduce_fusion.1
  5.2 0.2 select_reduce_fusion
  5.5 0.1 div.34
  5.5 2.4 %fusion.4 = bf16[320,1440]{1,0:T(8,128)(2,1)} fusion(pred[128,320]{0,1:T(32,128)(4,1)S(1)} %bitcast_compare_fusion, bf16[128,1440]{0,1:T(8,128)(2,1)} %param.15, f32[320]{0:T(512)S(1)} %div.34), kind=kOutput, calls=%fused_computation.11 | convolution fusion | flops 118886400 | bytes 1332480 | tf_op jit(solution)/shard_map/dot_general | solution.py:23
  7.9 59.7 %inbound.1 = (bf16[2,8,40,1440]{3,2,1,0:T(8,128)(2,1)}, bf16[2,8,40,1440]{3,2,1,0:T(8,128)(2,1)}, bf16[1440,360]{1,0:T(8,128)(2,1)}, bf16[360,1440]{1,0:T(8,128)(2,1)}) custom-call(bf16[8,40,1440]{2,1,0:T(8,128)(2,1)} %bitcast.66, bf16[8,40,1440]{2,1,0:T(8,128)(2,1)} %bitcast.67, bf16[1440,360]{1,0:T(8,128)(2,1)} %bitcast.65, bf16[360,1440]{1,0:T(8,128)(2,1)} %bitcast.68), custom_call_target="tpu_custom_call" | custom-call | tf_op jit(solution)/shard_map/inbound/pallas_call | solution.py:220
  67.7 0.0 copy-done.1
  67.7 0.0 copy-start.2
  67.7 2.7 %fusion.46 = f32[640,360]{0,1:T(8,128)S(1)} fusion(bf16[640,1440]{1,0:T(8,128)(2,1)} %bitcast.73, bf16[1,1440,360]{2,1,0:T(8,128)(2,1)S(1)} %copy-done.1), kind=kOutput, calls=%fused_computation.79 | convolution fusion | flops 663552000 | bytes 3801600 | tf_op jit(solution)/shard_map/dot_general | solution.py:23
  70.4 0.0 copy-done.2
  70.4 0.0 copy-start.19
  70.4 0.0 copy-start.3
  70.4 0.0 copy-start.10
  70.4 1.3 fusion.42
  71.8 0.0 copy-done.19
  71.8 0.2 copy-done.3
  72.0 0.6 copy-done.10
  72.6 1.1 fusion.56
  73.7 0.0 copy-start.16
  73.7 0.9 copy-done.16
  74.7 1.4 fusion
  76.1 2.5 %copy.16 = bf16[640,1440]{1,0:T(8,128)(2,1)} copy(bf16[640,1440]{0,1:T(8,128)(2,1)S(1)} %fusion) | data formatting | bytes 3686400 | tf_op jit(solution)/shard_map/convert_element_type | solution.py:295
  78.5 3.2 %fusion.12 = bf16[640,360]{0,1:T(8,128)(2,1)S(1)} fusion(bf16[640,1440]{1,0:T(8,128)(2,1)} %bitcast.69, f32[640,360]{0,1:T(8,128)} %copy-done.19, bf16[1,360,1440]{2,1,0:T(8,128)(2,1)} %param.14), kind=kOutput, calls=%fused_computation.25 | convolution fusion | flops 665856000 | bytes 4262400 | tf_op jit(solution)/shard_map/dot_general | solution.py:23
  81.8 0.0 copy-start.17
  81.8 1.2 fusion.44
  83.0 0.3 copy-done.7
  83.3 0.3 copy-done.15
  83.6 0.3 copy-done.17
  83.9 1.1 fusion.13
  85.0 0.1 copy-done.4
  85.1 1.4 fusion.1
  86.5 2.5 %copy.17 = bf16[640,1440]{1,0:T(8,128)(2,1)} copy(bf16[640,1440]{0,1:T(8,128)(2,1)S(1)} %fusion.1) | data formatting | bytes 3686400 | tf_op jit(solution)/shard_map/convert_element_type | solution.py:296
  88.9 4.0 %convolution_convert_fusion.refs_2_ = bf16[1440,360]{1,0:T(8,128)(2,1)} fusion(bf16[640,1440]{1,0:T(8,128)(2,1)} %bitcast.74, bf16[640,360]{0,1:T(8,128)(2,1)S(1)} %fusion.13), kind=kOutput, calls=%fused_computation.8 | convolution fusion | flops 664070400 | bytes 3340800 | tf_op jit(solution)/shard_map/dot_general | solution.py:23
  92.9 2.0 %convolution_convert_fusion.1.refs_3_ = bf16[360,1440]{1,0:T(8,128)(2,1)} fusion(bf16[640,1440]{1,0:T(8,128)(2,1)S(1)} %bitcast.71, f32[640,360]{0,1:T(8,128)S(1)} %copy-done.18), kind=kOutput, calls=%fused_computation.10 | convolution fusion | flops 665452800 | bytes 3801600 | tf_op jit(solution)/shard_map/dot_general | solution.py:23
  95.0 53.6 %outbound.1 = (bf16[8,40,1440]{2,1,0:T(8,128)(2,1)}, bf16[8,40,1440]{2,1,0:T(8,128)(2,1)}, bf16[1440,360]{1,0:T(8,128)(2,1)}, bf16[360,1440]{1,0:T(8,128)(2,1)}) custom-call(bf16[2,8,40,1440]{3,2,1,0:T(8,128)(2,1)} %bitcast.63, bf16[2,8,40,1440]{3,2,1,0:T(8,128)(2,1)} %bitcast.64, bf16[1440,360]{1,0:T(8,128)(2,1)} %convolution_convert_fusion.refs_2_, ...), custom_call_target="tpu_custom_call" | custom-call | tf_op jit(solution)/shard_map/outbound/pallas_call | solution.py:241
  148.6 1.9 %fusion.9 = f32[128,1440]{0,1:T(8,128)S(1)} fusion(bf16[8,40,1440]{2,1,0:T(8,128)(2,1)} %get-tuple-element.16, s32[128,8]{0,1:T(8,128)S(1)} %select_reduce_fusion.1, s32[128,8]{0,1:T(8,128)S(1)} %and_select_fusion), kind=kOutput, calls=%fused_computation.20 | convolution fusion | flops 118886400 | bytes 1667072 | tf_op jit(solution)/shard_map/dot_general | solution.py:23
  150.6 1.3 fusion.10
  151.9 1.3 fusion.11
  153.3 2.3 %fusion.5 = bf16[1,1440,360]{2,1,0:T(8,128)(2,1)} fusion(bf16[640,1440]{1,0:T(8,128)(2,1)S(1)} %bitcast.76, bf16[640,360]{0,1:T(8,128)(2,1)S(1)} %fusion.12, bf16[1440,360]{1,0:T(8,128)(2,1)S(1)} %copy-done.13), kind=kOutput, calls=%fused_computation.13 | convolution fusion | flops 665107200 | bytes 4377600 | tf_op jit(solution)/shard_map/dot_general | solution.py:23
  155.6 0.0 copy-done.20
  155.6 2.1 %fusion.6 = bf16[1,360,1440]{2,1,0:T(8,128)(2,1)} fusion(bf16[640,1440]{1,0:T(8,128)(2,1)S(1)} %bitcast.72, bf16[360,1440]{1,0:T(8,128)(2,1)S(1)} %copy-done.12, f32[640,360]{0,1:T(8,128)S(1)} %copy-done.20), kind=kOutput, calls=%fused_computation.14 | convolution fusion | flops 666489600 | bytes 4838400 | tf_op jit(solution)/shard_map/dot_general | solution.py:23
  (27 shorter events, 0.1 us)
Async XLA Ops:
  0.6 2.5 %copy-start = (bf16[128,1440]{0,1:T(8,128)(2,1)S(1)}, bf16[128,1440]{0,1:T(8,128)(2,1)}, u32[]{:S(2)}) copy-start(bf16[128,1440]{0,1:T(8,128)(2,1)} %param.8) | copy-start | bytes 1105924
  7.9 59.7 %copy-start.1 = (bf16[1,1440,360]{2,1,0:T(8,128)(2,1)S(1)}, bf16[1,1440,360]{2,1,0:T(8,128)(2,1)}, u32[]{:S(2)}) copy-start(bf16[1,1440,360]{2,1,0:T(8,128)(2,1)} %param.13) | copy-start | bytes 3110404
  67.7 2.7 %copy-start.2 = (bf16[1,360,1440]{2,1,0:T(8,128)(2,1)S(1)}, bf16[1,360,1440]{2,1,0:T(8,128)(2,1)}, u32[]{:S(2)}) copy-start(bf16[1,360,1440]{2,1,0:T(8,128)(2,1)} %param.14) | copy-start | bytes 3110404
  70.4 1.4 copy-start.19
  70.4 1.6 %copy-start.3 = (bf16[1440,360]{1,0:T(8,128)(2,1)S(1)}, bf16[1440,360]{1,0:T(8,128)(2,1)}, u32[]{:S(2)}) copy-start(bf16[1440,360]{1,0:T(8,128)(2,1)} %get-tuple-element.13) | copy-start | bytes 3110404
  70.4 2.2 %copy-start.10 = (bf16[2,8,40,1440]{3,2,1,0:T(8,128)(2,1)S(1)}, bf16[2,8,40,1440]{3,2,1,0:T(8,128)(2,1)}, u32[]{:S(2)}) copy-start(bf16[2,8,40,1440]{3,2,1,0:T(8,128)(2,1)} %get-tuple-element.12) | copy-start | bytes 5529604
  72.6 2.0 %copy-start.14 = (bf16[360,1440]{1,0:T(8,128)(2,1)S(1)}, bf16[360,1440]{1,0:T(8,128)(2,1)}, u32[]{:S(2)}) copy-start(bf16[360,1440]{1,0:T(8,128)(2,1)} %get-tuple-element.14) | copy-start | bytes 3110404
  73.7 0.9 copy-start.16
  81.8 1.5 copy-start.7
  81.8 1.8 %copy-start.15 = (bf16[360,1440]{1,0:T(8,128)(2,1)S(1)}, bf16[360,1440]{1,0:T(8,128)(2,1)}, u32[]{:S(2)}) copy-start(bf16[360,1440]{1,0:T(8,128)(2,1)} %get-tuple-element.14) | copy-start | bytes 3110404
  81.8 2.1 %copy-start.17 = (f32[640,360]{0,1:T(8,128)S(1)}, f32[640,360]{0,1:T(8,128)}, u32[]{:S(2)}) copy-start(f32[640,360]{0,1:T(8,128)} %copy-done.16) | copy-start | bytes 2764804
  83.9 1.2 copy-start.4
  88.9 4.0 %copy-start.8 = (bf16[2,8,40,1440]{3,2,1,0:T(8,128)(2,1)S(1)}, bf16[2,8,40,1440]{3,2,1,0:T(8,128)(2,1)}, u32[]{:S(2)}) copy-start(bf16[2,8,40,1440]{3,2,1,0:T(8,128)(2,1)} %get-tuple-element.15) | copy-start | bytes 5529604
  88.9 4.0 %copy-start.18 = (f32[640,360]{0,1:T(8,128)S(1)}, f32[640,360]{0,1:T(8,128)}, u32[]{:S(2)}) copy-start(f32[640,360]{0,1:T(8,128)} %copy-done.16) | copy-start | bytes 2764804
  148.6 2.0 %copy-start.6 = (bf16[8,40,1440]{2,1,0:T(8,128)(2,1)S(1)}, bf16[8,40,1440]{2,1,0:T(8,128)(2,1)}, u32[]{:S(2)}) copy-start(bf16[8,40,1440]{2,1,0:T(8,128)(2,1)} %get-tuple-element.16) | copy-start | bytes 2764804
  148.6 3.3 %copy-start.5 = (bf16[8,40,1440]{2,1,0:T(8,128)(2,1)S(1)}, bf16[8,40,1440]{2,1,0:T(8,128)(2,1)}, u32[]{:S(2)}) copy-start(bf16[8,40,1440]{2,1,0:T(8,128)(2,1)} %get-tuple-element.17) | copy-start | bytes 2764804
  150.6 2.7 %copy-start.11 = (bf16[2,8,40,1440]{3,2,1,0:T(8,128)(2,1)S(1)}, bf16[2,8,40,1440]{3,2,1,0:T(8,128)(2,1)}, u32[]{:S(2)}) copy-start(bf16[2,8,40,1440]{3,2,1,0:T(8,128)(2,1)} %get-tuple-element.12) | copy-start | bytes 5529604
  150.6 2.7 %copy-start.13 = (bf16[1440,360]{1,0:T(8,128)(2,1)S(1)}, bf16[1440,360]{1,0:T(8,128)(2,1)}, u32[]{:S(2)}) copy-start(bf16[1440,360]{1,0:T(8,128)(2,1)} %get-tuple-element.18) | copy-start | bytes 3110404
  153.3 2.3 %copy-start.9 = (bf16[2,8,40,1440]{3,2,1,0:T(8,128)(2,1)S(1)}, bf16[2,8,40,1440]{3,2,1,0:T(8,128)(2,1)}, u32[]{:S(2)}) copy-start(bf16[2,8,40,1440]{3,2,1,0:T(8,128)(2,1)} %get-tuple-element.15) | copy-start | bytes 5529604
  153.3 2.3 %copy-start.12 = (bf16[360,1440]{1,0:T(8,128)(2,1)S(1)}, bf16[360,1440]{1,0:T(8,128)(2,1)}, u32[]{:S(2)}) copy-start(bf16[360,1440]{1,0:T(8,128)(2,1)} %get-tuple-element.19) | copy-start | bytes 3110404
  153.3 2.3 %copy-start.20 = (f32[640,360]{0,1:T(8,128)S(1)}, f32[640,360]{0,1:T(8,128)}, u32[]{:S(2)}) copy-start(f32[640,360]{0,1:T(8,128)} %copy-done.19) | copy-start | bytes 2764804
